TPU v7x, 512 devices: a whole 4x4x16 slice. The times are simulated.
512 devices in a mesh: dp: 32 (over y, x, core), expert: 16 (over z).
Axes of the slice: x: 4, y: 4, z: 16, core: 2. Of those that a mesh axis runs over, the one named last changes fastest.
Arguments:
- enc_out: bfloat16 [65536, 1408], P(('dp', 'expert')), may hold values from -40 to 40
- actions: int32 [65536], P(('dp', 'expert')), may hold values from 0 to 255
- enc_gain: float32 [1408], replicated, may hold values from 0.1 to 1.9
- enc_bias: float32 [1408], replicated, may hold values from -4 to 4
- embed_w: bfloat16 [1408, 1024], replicated, may hold values from -0.15625 to 0.15625
- action_table: bfloat16 [256, 1024], replicated, may hold values from -6 to 6
- pred_gain: float32 [1024], replicated, may hold values from 0.1 to 1.9
- router_w: bfloat16 [1024, 32], replicated, may hold values from -0.1875 to 0.1875
- up_w: bfloat16 [32, 1024, 768], P('expert', 'dp'), may hold values from -0.1875 to 0.1875
- down_w: bfloat16 [32, 768, 1024], P('expert', 'dp'), may hold values from -0.21875 to 0.21875
- cotangent: bfloat16 [65536, 1024], P(('dp', 'expert')), may hold values from -0.5 to 0.5
- routes: int32 [65536, 6], P(('dp', 'expert')), may hold values from 0 to 31, all different within a row; in each aligned block of 128 rows (0 to 127, 128 to 255, ...) at most 32 rows name the same one
Outputs:
- predicted: bfloat16 [65536, 1024], P(('dp', 'expert'))
- grad_down: bfloat16 [32, 768, 1024], P('expert', 'dp')
Inputs may be any that keep to these rules, and one draw needn't show every extreme that they name: `routes`: within the 128 rows of one device each expert is named by at most 32 rows, a bound that some expert reaches in every such block.
All inputs are finite; a program needn't handle non-finite values.
Results may differ from a plain program's by a relative error of at most 0.017.
Values may be sent and summed in bfloat16 or wider, within the bound.
No kernel may reach another device: no remote copies, remote signals or barrier semaphores. Data moves between devices by JAX's collectives and lax.ppermute only.
A program may use at most 64 MiB of HBM per device.

v0:
```python
import jax
import jax.numpy as jnp
from jax import lax
from jax.sharding import PartitionSpec as P

EXPERTS = 32
TOPK = 6
CAP = 32


def per_device(
    enc_out,
    actions,
    enc_gain,
    enc_bias,
    embed_w,
    action_table,
    pred_gain,
    router_w,
    up_w,
    down_w,
    cotangent,
    routes,
):
    tok_rows = enc_out.shape[0]
    encoded = enc_out.astype(jnp.float32)
    center = encoded - jnp.mean(encoded, axis=-1, keepdims=True)
    spread = jnp.mean(center * center, axis=-1, keepdims=True)
    normed = (center * lax.rsqrt(spread + 1e-06) * enc_gain + enc_bias).astype(jnp.bfloat16)
    onehot = (
        actions[:, None] == jnp.arange(action_table.shape[0], dtype=jnp.int32)[None, :]
    ).astype(jnp.bfloat16)
    residual = jnp.dot(normed, embed_w, preferred_element_type=jnp.float32) + jnp.dot(
        onehot, action_table, preferred_element_type=jnp.float32
    )
    scaled = (
        residual
        * lax.rsqrt(jnp.mean(residual * residual, axis=-1, keepdims=True) + 1e-06)
        * pred_gain
    ).astype(jnp.bfloat16)
    logits = jnp.dot(scaled, router_w, preferred_element_type=jnp.float32)
    gate_values = jax.nn.sigmoid(jnp.take_along_axis(logits, routes, axis=1))
    flat_routes = routes.reshape(-1)
    route_hits = (flat_routes[:, None] == jnp.arange(EXPERTS, dtype=jnp.int32)[None, :]).astype(
        jnp.int32
    )
    slot_rank = jnp.sum((jnp.cumsum(route_hits, axis=0) - route_hits) * route_hits, axis=1)
    position = flat_routes * CAP + slot_rank
    flat_gates = gate_values.reshape(-1)
    model_width = scaled.shape[1]
    owners = lax.axis_size("expert")
    per_owner = EXPERTS // owners
    token_rep = jnp.repeat(scaled, TOPK, axis=0)
    grad_rep = (
        flat_gates[:, None] * jnp.repeat(cotangent, TOPK, axis=0).astype(jnp.float32)
    ).astype(jnp.bfloat16)
    send_tokens = jnp.zeros((EXPERTS * CAP, model_width), jnp.bfloat16).at[position].set(token_rep)
    send_grads = jnp.zeros((EXPERTS * CAP, model_width), jnp.bfloat16).at[position].set(grad_rep)
    send_tokens = send_tokens.reshape(owners, per_owner * CAP, model_width)
    send_grads = send_grads.reshape(owners, per_owner * CAP, model_width)
    got_tokens, got_grads = (
        lax.all_to_all(send_tokens, "expert", split_axis=0, concat_axis=0, tiled=True),
        lax.all_to_all(send_grads, "expert", split_axis=0, concat_axis=0, tiled=True),
    )
    got_grads = got_grads.reshape(owners, per_owner, CAP, model_width)
    got_tokens = got_tokens.reshape(owners, per_owner, CAP, model_width)
    pre_act = jnp.einsum(
        "secd,edh->sech",
        got_tokens,
        lax.all_gather(up_w, "dp", axis=1, tiled=True),
        preferred_element_type=jnp.float32,
    )
    hidden = jax.nn.gelu(pre_act, approximate=True).astype(jnp.bfloat16)
    hidden_part = hidden
    expert_out = jnp.einsum(
        "sech,ehd->secd",
        hidden_part,
        lax.all_gather(down_w, "dp", axis=1, tiled=True),
        preferred_element_type=jnp.float32,
    )
    expert_out = expert_out.astype(jnp.bfloat16).reshape(owners, per_owner * CAP, model_width)
    returned = lax.all_to_all(
        expert_out, "expert", split_axis=0, concat_axis=0, tiled=True
    ).reshape(EXPERTS * CAP, model_width)
    picked = returned[position].astype(jnp.float32) * flat_gates[:, None]
    predicted = (residual + jnp.sum(picked.reshape(tok_rows, TOPK, model_width), axis=1)).astype(
        jnp.bfloat16
    )
    hidden_part = hidden
    summed = lax.psum_scatter(
        jnp.einsum(
            "sech,secd->hed", hidden_part, got_grads, preferred_element_type=jnp.float32
        ).astype(jnp.bfloat16),
        "dp",
        scatter_dimension=0,
        tiled=True,
    ).astype(jnp.float32)
    grad_down = jnp.transpose(summed, (1, 0, 2)).astype(jnp.bfloat16)
    return (predicted, grad_down)


def solution(mesh):
    placed = (
        P(("dp", "expert"), None),
        P(("dp", "expert")),
        P(),
        P(),
        P(),
        P(),
        P(),
        P(),
        P("expert", "dp", None),
        P("expert", "dp", None),
        P(("dp", "expert"), None),
        P(("dp", "expert"), None),
    )
    return jax.shard_map(
        per_device,
        mesh=mesh,
        in_specs=placed,
        out_specs=(P(("dp", "expert"), None), P("expert", "dp", None)),
        check_vma=False,
    )
```

profile of v0, /device:TPU:6, one launch (start us, length us, event | category | flops | bytes accessed | tf_op | source)
XLA Modules:
  0.0 437.3 jit_solution(1082023896010082765)
XLA Ops:
  12.8 1.7 multiply_reduce_fusion.1
  15.4 1.6 broadcast_in_dim.7
  17.0 3.7 reshape.164
  21.4 3.3 reduce-window.6
  26.8 8.0 %scatter_custom_fusion = bf16[1024,1024]{1,0:T(8,128)(2,1)} fusion(s32[768]{0:T(1024)S(1)} %fusion.43, bf16[768,1024]{1,0:T(8,128)(2,1)} %reshape.164, bf16[]{:T(256)} %constant.17.clone.1), kind=kCustom, calls=%fused_computation.28 | custom fusion | bytes 2097664 | tf_op jit(solution)/shard_map/scatter | solution.py:57
  34.8 15.4 %all-to-all-start = ((bf16[16,64,1024]{2,1,0:T(8,128)(2,1)}), bf16[16,64,1024]{2,1,0:T(8,128)(2,1)}, u32[]{:S(2)}, u32[]{:S(2)}) async-start(bf16[16,64,1024]{2,1,0:T(8,128)(2,1)} %bitcast.64), calls=%async_computation | async-start | bytes 4194304 | tf_op jit(solution)/shard_map/all_to_all | solution.py:62
  52.4 5.1 %gather_fusion.1 = f32[768]{0:T(1024)S(1)} fusion(f32[128,32]{0,1:T(8,128)S(1)} %fusion.44, s32[768]{0:T(1024)S(1)} %reshape.154), kind=kCustom, calls=%fused_computation.1 | custom fusion | bytes 12288 | tf_op jit(solution)/shard_map/jit(take_along_axis)/gather | solution.py:42
  58.0 3.4 broadcast_in_dim.10
  61.4 4.7 %convert_element_type.69 = f32[768,1024]{1,0:T(8,128)} reshape(f32[128,6,1024]{2,1,0:T(8,128)} %broadcast_in_dim.10) | data formatting | bytes 6291456 | tf_op jit(solution)/shard_map/convert_element_type | solution.py:55
  66.2 11.3 %scatter_custom_fusion.1 = bf16[1024,1024]{1,0:T(8,128)(2,1)} fusion(s32[768]{0:T(1024)S(1)} %fusion.43, f32[768,1024]{1,0:T(8,128)} %convert_element_type.69, f32[768]{0:T(1024)S(1)} %reshape.145, bf16[]{:T(256)} %constant.17.clone.1), kind=kCustom, calls=%fused_computation.23 | custom fusion | flops 1572864 | bytes 5246978 | tf_op jit(solution)/shard_map/scatter | solution.py:58
  77.5 68.2 %all-to-all-done = bf16[16,64,1024]{2,1,0:T(8,128)(2,1)} async-done(((bf16[16,64,1024]{2,1,0:T(8,128)(2,1)}), bf16[16,64,1024]{2,1,0:T(8,128)(2,1)}, u32[]{:S(2)}, u32[]{:S(2)}) %all-to-all-start) | async-done | bytes 2097184 | tf_op jit(solution)/shard_map/all_to_all | solution.py:62
  145.7 7.5 %all-to-all-start.2 = ((bf16[16,64,1024]{2,1,0:T(8,128)(2,1)}), bf16[16,64,1024]{2,1,0:T(8,128)(2,1)}, u32[]{:S(2)}, u32[]{:S(2)}) async-start(bf16[16,64,1024]{2,1,0:T(8,128)(2,1)} %bitcast.65), calls=%async_computation.2 | async-start | bytes 4194304 | tf_op jit(solution)/shard_map/all_to_all | solution.py:63
  153.9 6.0 %fusion.7 = bf16[16,2,32,768]{3,2,0,1:T(8,128)(2,1)} fusion(bf16[2,1024,768]{2,1,0:T(8,128)(2,1)} %all-gather.3.cloned.1.call-done, bf16[16,2,32,1024]{3,2,1,0:T(8,128)(2,1)} %bitcast.2), kind=kOutput, calls=%fused_computation.14 | convolution fusion | flops 1617690624 | bytes 6815744 | tf_op jit(solution)/shard_map/secd,edh->sech/dot_general | solution.py:67
  159.9 58.3 %all-gather.5.cloned.1.call-done = bf16[2,768,1024]{2,1,0:T(8,128)(2,1)} async-done(((bf16[2,24,1024]{2,1,0:T(8,128)(2,1)}), bf16[2,768,1024]{2,1,0:T(8,128)(2,1)}) %all-gather.5.cloned.1.call-update) | async-done | bytes 3145744 | tf_op jit(solution)/shard_map/all_gather | solution.py:78
  218.2 4.2 convert_bitcast_fusion
  222.4 1.5 copy.48
  223.8 24.6 %all-to-all-done.2 = bf16[16,64,1024]{2,1,0:T(8,128)(2,1)} async-done(((bf16[16,64,1024]{2,1,0:T(8,128)(2,1)}), bf16[16,64,1024]{2,1,0:T(8,128)(2,1)}, u32[]{:S(2)}, u32[]{:S(2)}) %all-to-all-start.2) | async-done | bytes 2097184 | tf_op jit(solution)/shard_map/all_to_all | solution.py:63
  248.5 7.8 %all-to-all-start.1 = ((bf16[16,64,1024]{2,1,0:T(8,128)(2,1)}), bf16[16,64,1024]{2,1,0:T(8,128)(2,1)}, u32[]{:S(2)}, u32[]{:S(2)}) async-start(bf16[16,64,1024]{2,1,0:T(8,128)(2,1)} %bitcast.63), calls=%async_computation.1 | async-start | bytes 4194304 | tf_op jit(solution)/shard_map/all_to_all | solution.py:82
  256.6 5.6 %fusion.8 = bf16[768,2,1024]{0,2,1:T(8,128)(2,1)} fusion(bf16[16,2,32,1024]{3,2,1,0:T(8,128)(2,1)} %bitcast.13, bf16[16,2,32,768]{3,2,0,1:T(8,128)(2,1)} %fusion.7), kind=kOutput, calls=%fused_computation.15 | convolution fusion | flops 1612185600 | bytes 6815744 | tf_op jit(solution)/shard_map/sech,secd->hed/dot_general | solution.py:91
  262.2 8.7 %copy.54 = bf16[768,2,1024]{2,1,0:T(2,128)(2,1)} copy(bf16[768,2,1024]{0,2,1:T(8,128)(2,1)} %fusion.8) | data formatting | bytes 6291456 | tf_op jit(solution)/shard_map/convert_element_type | solution.py:93
  272.9 141.6 %all-reduce.3.cloned.1.call-done = bf16[768,2,1024]{2,1,0:T(2,128)(2,1)} async-done(((bf16[768,2,1024]{2,1,0:T(2,128)(2,1)}), bf16[768,2,1024]{2,1,0:T(2,128)(2,1)}) %all-reduce.3.cloned.1.call-update) | async-done | bytes 3145744
  416.1 6.4 %gather_fusion = bf16[768,1024]{1,0:T(8,128)(2,1)} fusion(bf16[1024,1024]{1,0:T(8,128)(2,1)} %bitcast.10, s32[1024]{0:T(1024)S(1)} %pad_clamp_fusion), kind=kCustom, calls=%fused_computation | custom fusion | bytes 3148800 | tf_op jit(solution)/shard_map/gather | solution.py:85
  422.5 3.9 reshape.143
  426.4 3.6 multiply_reduce_fusion
  (48 shorter events, 16.5 us)
Async XLA Ops:
  7.2 5.6 %copy-start = (bf16[1408,1024]{1,0:T(8,128)(2,1)S(1)}, bf16[1408,1024]{1,0:T(8,128)(2,1)}, u32[]{:S(2)}) copy-start(bf16[1408,1024]{1,0:T(8,128)(2,1)} %param.16) | copy-start | bytes 8650756
  12.8 1.8 copy-start.3
  14.7 0.7 copy-start.1
  34.8 16.1 %copy-start.2 = (s32[128,6]{0,1:T(8,128)S(1)}, s32[128,6]{0,1:T(8,128)}, u32[]{:S(2)}) copy-start(s32[128,6]{0,1:T(8,128)} %param.23) | copy-start | bytes 9220
  34.8 110.9 %all-to-all-start = ((bf16[16,64,1024]{2,1,0:T(8,128)(2,1)}), bf16[16,64,1024]{2,1,0:T(8,128)(2,1)}, u32[]{:S(2)}, u32[]{:S(2)}) async-start(bf16[16,64,1024]{2,1,0:T(8,128)(2,1)} %bitcast.64), calls=%async_computation | async-start | bytes 4194304 | tf_op jit(solution)/shard_map/all_to_all | solution.py:62
  50.2 103.7 %all-gather.3.cloned.1.call-start = ((), (), s32[]{:S(2)}) async-start(), calls=%async_computation.3 | async-start | bytes 3244032 | tf_op jit(solution)/shard_map/all_gather | solution.py:70
  145.7 102.8 %all-to-all-start.2 = ((bf16[16,64,1024]{2,1,0:T(8,128)(2,1)}), bf16[16,64,1024]{2,1,0:T(8,128)(2,1)}, u32[]{:S(2)}, u32[]{:S(2)}) async-start(bf16[16,64,1024]{2,1,0:T(8,128)(2,1)} %bitcast.65), calls=%async_computation.2 | async-start | bytes 4194304 | tf_op jit(solution)/shard_map/all_to_all | solution.py:63
  153.2 65.0 %all-gather.5.cloned.1.call-start = ((), (), s32[]{:S(2)}) async-start(), calls=%async_computation.4 | async-start | bytes 3244032 | tf_op jit(solution)/shard_map/all_gather | solution.py:78
  248.5 167.7 %all-to-all-start.1 = ((bf16[16,64,1024]{2,1,0:T(8,128)(2,1)}), bf16[16,64,1024]{2,1,0:T(8,128)(2,1)}, u32[]{:S(2)}, u32[]{:S(2)}) async-start(bf16[16,64,1024]{2,1,0:T(8,128)(2,1)} %bitcast.63), calls=%async_computation.1 | async-start | bytes 4194304 | tf_op jit(solution)/shard_map/all_to_all | solution.py:82
  256.3 158.2 %all-reduce.3.cloned.1.call-start = ((), (), s32[]{:S(2)}) async-start(), calls=%async_computation.5 | async-start | bytes 6291456
Sparse Core Ops, SparseCore 0:
  54.2 61.0 all-gather.2
  157.1 61.0 all-gather.4
  271.1 143.3 all-reduce.2
where the time goes:
time: 439 us; the launch traced here: 437 us
  waiting for transfers between devices  294 us (67%)
  local copies, waits for them, and re-layouts  54.6 us (12%)
  starting transfers between devices  31.2 us (7%)
  other arithmetic  22.9 us (5%)
  matrix products  19.9 us (5%)
  between operations  14.6 us (3%)
    unnamed x4, waiting for transfers between devices  143 us
    all_to_all x1, waiting for transfers between devices, per_device(): lax.all_to_all(send_tokens, 'expert', split_axis=0, concat_axis=0, tiled=...  68.2 us
    all_gather x1, waiting for transfers between devices, per_device(): lax.all_gather(down_w, 'dp', axis=1, tiled=True)  58.3 us
    all_to_all x1, waiting for transfers between devices, per_device(): lax.all_to_all(send_grads, 'expert', split_axis=0, concat_axis=0, tiled=T...  24.6 us
    all_to_all x1, starting transfers between devices, per_device(): lax.all_to_all(send_tokens, 'expert', split_axis=0, concat_axis=0, tiled=...  15.4 us
    scatter x1, other arithmetic, per_device(): jnp.zeros((EXPERTS * CAP, model_width), jnp.bfloat16).at[position]  11.3 us
  transfers between devices with their start and end apart: 6, of which 4 were waited for; matrix products, arithmetic and copies ran while one was open for 13% of the time, Pallas kernels for 0%

commit v1 on v0

v1 whole, which is shorter than its diff:
```python
import jax
import jax.numpy as jnp
from jax import lax
from jax.sharding import PartitionSpec as P

EXPERTS = 32
TOPK = 6
CAP = 32


def exchange(rows):
    return lax.all_to_all(rows, "dp", split_axis=0, concat_axis=0, tiled=True)


def swap(pair):
    planes, chips = lax.axis_size("expert"), lax.axis_size("dp") // 2
    odd = lax.axis_index("dp") % 2 == 1
    same, other = jnp.where(odd, pair[1], pair[0]), jnp.where(odd, pair[0], pair[1])
    moved = []
    for flip, rows in ((0, same), (1, other)):
        perm = [
            ((2 * chip + core) * planes + z, (2 * z + (core ^ flip)) * planes + chip)
            for chip in range(chips)
            for core in range(2)
            for z in range(planes)
        ]
        moved.append(lax.ppermute(rows, ("dp", "expert"), perm))
    same, other = moved
    return jnp.stack([jnp.where(odd, other, same), jnp.where(odd, same, other)])


def per_device(
    enc_out,
    actions,
    enc_gain,
    enc_bias,
    embed_w,
    action_table,
    pred_gain,
    router_w,
    up_w,
    down_w,
    cotangent,
    routes,
):
    bf16, f32 = jnp.bfloat16, jnp.float32
    tokens, width = cotangent.shape
    hid_rows, up_cols = down_w.shape[1], up_w.shape[2]
    up_rows = up_w.shape[1]
    packed = jnp.concatenate(
        [jnp.pad(up_w, ((0, 0), (0, 0), (0, width - up_cols))), down_w], axis=1
    )
    weights = lax.all_gather(swap(packed), "expert", axis=0, tiled=True)
    up = weights[:, :up_rows, :up_cols].reshape(width, up_cols)
    down = weights[:, up_rows:, :].reshape(up_cols, width)

    experts = jnp.arange(EXPERTS, dtype=jnp.int32)
    hits = jnp.sum((routes.T[:, None, :] == experts[None, :, None]).astype(f32), axis=0)
    order = jnp.arange(tokens, dtype=jnp.int32)
    earlier = (order[:, None] < order[None, :]).astype(bf16)
    rank = jnp.dot(hits.astype(bf16), earlier, preferred_element_type=f32)
    place = jnp.where(hits > 0.0, rank.astype(jnp.int32), -1)
    slots = jnp.arange(CAP, dtype=jnp.int32)
    pick = (place[:, None, :] == slots[None, :, None]).reshape(EXPERTS * CAP, tokens)
    pick = pick.astype(bf16)

    got_cot = exchange(jnp.dot(pick, cotangent, preferred_element_type=f32).astype(bf16))

    encoded = enc_out.astype(f32)
    center = encoded - jnp.mean(encoded, axis=-1, keepdims=True)
    spread = jnp.mean(center * center, axis=-1, keepdims=True)
    normed = (center * lax.rsqrt(spread + 1e-06) * enc_gain + enc_bias).astype(bf16)
    onehot = (
        actions[:, None] == jnp.arange(action_table.shape[0], dtype=jnp.int32)[None, :]
    ).astype(bf16)
    residual = jnp.dot(normed, embed_w, preferred_element_type=f32) + jnp.dot(
        onehot, action_table, preferred_element_type=f32
    )
    scaled = (
        residual
        * lax.rsqrt(jnp.mean(residual * residual, axis=-1, keepdims=True) + 1e-06)
        * pred_gain
    ).astype(bf16)
    gates = jax.nn.sigmoid(
        lax.dot_general(
            router_w, scaled, (((0,), (1,)), ((), ())), preferred_element_type=f32
        )
    )
    got_tok = exchange(jnp.dot(pick, scaled, preferred_element_type=f32).astype(bf16))

    pre = jnp.dot(got_tok, up, preferred_element_type=f32)
    hidden = jax.nn.gelu(pre, approximate=True).astype(bf16)
    mine = experts == lax.axis_index("dp")
    all_gates = jax.nn.sigmoid(jnp.dot(got_tok, router_w, preferred_element_type=f32))
    gate = jnp.sum(jnp.where(mine[None, :], all_gates, 0.0), axis=1, keepdims=True)
    gated = (gate * got_cot.astype(f32)).astype(bf16)
    grad = lax.dot_general(
        hidden, gated, (((0,), (0,)), ((), ())), preferred_element_type=f32
    ).astype(bf16)
    summed = lax.psum_scatter(grad, "expert", scatter_dimension=0, tiled=True)
    grad_down = swap(summed.reshape(2, hid_rows, width))

    expert_out = jnp.dot(hidden, down, preferred_element_type=f32).astype(bf16)
    returned = exchange(expert_out)
    weight = pick.reshape(EXPERTS, CAP, tokens).astype(f32) * gates[:, None, :]
    weight = weight.reshape(EXPERTS * CAP, tokens)
    coarse = weight.astype(bf16)
    fine = (weight - coarse.astype(f32)).astype(bf16)
    dims = (((0,), (0,)), ((), ()))
    combined = lax.dot_general(
        coarse, returned, dims, preferred_element_type=f32
    ) + lax.dot_general(fine, returned, dims, preferred_element_type=f32)
    predicted = (residual + combined).astype(bf16)
    return (predicted, grad_down)


def solution(mesh):
    placed = (
        P(("dp", "expert"), None),
        P(("dp", "expert")),
        P(),
        P(),
        P(),
        P(),
        P(),
        P(),
        P("expert", "dp", None),
        P("expert", "dp", None),
        P(("dp", "expert"), None),
        P(("dp", "expert"), None),
    )
    return jax.shard_map(
        per_device,
        mesh=mesh,
        in_specs=placed,
        out_specs=(P(("dp", "expert"), None), P("expert", "dp", None)),
        check_vma=False,
    )
```

time: 439 us -> 261 us (0.59)
  the two profiles are of different devices: /device:TPU:6 before, /device:TPU:81 now
where the time goes in v1:
time: 261 us; the launch traced here: 260 us
  waiting for transfers between devices  118 us (45%)
  starting transfers between devices  86 us (33%)
  matrix products  33.1 us (13%)
  between operations  14.3 us (5%)
  other arithmetic  5.66 us (2%)
  local copies, waits for them, and re-layouts  3.04 us (1%)
    all_to_all x3, waiting for transfers between devices, exchange(): return lax.all_to_all(rows, 'dp', split_axis=0, concat_axis=0, tiled=True)  52.3 us
    ppermute x4, starting transfers between devices, swap(): moved.append(lax.ppermute(rows, ('dp', 'expert'), perm))  44.1 us
    all_to_all x3, starting transfers between devices, exchange(): return lax.all_to_all(rows, 'dp', split_axis=0, concat_axis=0, tiled=True)  41.8 us
    ppermute x4, waiting for transfers between devices, swap(): moved.append(lax.ppermute(rows, ('dp', 'expert'), perm))  28.9 us
    all_gather x1, waiting for transfers between devices, per_device(): weights = lax.all_gather(swap(packed), 'expert', axis=0, tiled=True)  22.4 us
    reduce_scatter x1, waiting for transfers between devices, per_device(): summed = lax.psum_scatter(grad, 'expert', scatter_dimension=0, tiled=True)  14.3 us
    dot_general x1, matrix products, per_device(): lax.dot_general(hidden, gated, (((0,), (0,)), ((), ())), preferred_elemen...  6 us
    dot_general x1, matrix products, per_device(): expert_out = jnp.dot(hidden, down, preferred_element_type=f32).astype(bf16)  5.35 us
  transfers between devices with their start and end apart: 9, of which 7 were waited for; matrix products, arithmetic and copies ran while one was open for 12% of the time, Pallas kernels for 0%

profile of v1, /device:TPU:81, one launch (start us, length us, event | category | flops | bytes accessed | tf_op | source)
XLA Modules:
  0.0 260.1 jit_solution(1251384041960015859)
XLA Ops:
  8.4 15.5 %collective-permute-start = (bf16[56,1024]{1,0:T(8,128)(2,1)S(1)}, bf16[56,1024]{1,0:T(8,128)(2,1)S(1)}, u32[]{:S(2)}, u32[]{:S(2)}) collective-permute-start(bf16[56,1024]{1,0:T(8,128)(2,1)S(1)} %get-tuple-element.4), channel_id=1, source_target_pairs={{0,16},{1,48},{2,80},{3,112},{4,144},{5,176},{6,208},{7,240},{8,27... | collective-permute-start | bytes 344072 | tf_op jit(solution)/shard_map/ppermute | solution.py:27
  23.9 2.0 collective-permute-start.1
  26.0 10.2 %collective-permute-done = bf16[56,1024]{1,0:T(8,128)(2,1)S(1)} collective-permute-done((bf16[56,1024]{1,0:T(8,128)(2,1)S(1)}, bf16[56,1024]{1,0:T(8,128)(2,1)S(1)}, u32[]{:S(2)}, u32[]{:S(2)}) %collective-permute-start) | collective-permute-done | bytes 114720 | tf_op jit(solution)/shard_map/ppermute | solution.py:27
  36.1 10.7 %collective-permute-done.1 = bf16[56,1024]{1,0:T(8,128)(2,1)S(1)} collective-permute-done((bf16[56,1024]{1,0:T(8,128)(2,1)S(1)}, bf16[56,1024]{1,0:T(8,128)(2,1)S(1)}, u32[]{:S(2)}, u32[]{:S(2)}) %collective-permute-start.1) | collective-permute-done | bytes 114720 | tf_op jit(solution)/shard_map/ppermute | solution.py:27
  51.4 1.7 multiply_reduce_fusion
  53.2 2.1 convolution_convert_fusion.1
  55.3 18.3 %all-to-all-start = ((bf16[32,32,1024]{2,1,0:T(8,128)(2,1)}), bf16[32,32,1024]{2,1,0:T(8,128)(2,1)}, u32[]{:S(2)}, u32[]{:S(2)}) async-start(bf16[32,32,1024]{2,1,0:T(8,128)(2,1)} %bitcast.49), calls=%async_computation | async-start | bytes 4194304 | tf_op jit(solution)/shard_map/all_to_all | solution.py:12
  73.6 3.0 %convolution_convert_fusion = bf16[1024,1024]{1,0:T(8,128)(2,1)} fusion(pred[1024,128]{1,0:T(32,128)(4,1)S(1)} %bitcast_compare_fusion, bf16[128,1024]{1,0:T(8,128)(2,1)} %param.22), kind=kOutput, calls=%fused_computation.13 | convolution fusion | flops 269484032 | bytes 2490368 | tf_op jit(solution)/shard_map/dot_general | solution.py:67
  76.7 24.7 %all-to-all-done = bf16[32,32,1024]{2,1,0:T(8,128)(2,1)} async-done(((bf16[32,32,1024]{2,1,0:T(8,128)(2,1)}), bf16[32,32,1024]{2,1,0:T(8,128)(2,1)}, u32[]{:S(2)}, u32[]{:S(2)}) %all-to-all-start) | async-done | bytes 2097184 | tf_op jit(solution)/shard_map/all_to_all | solution.py:12
  101.4 7.1 %all-to-all-start.2 = ((bf16[32,32,1024]{2,1,0:T(8,128)(2,1)}), bf16[32,32,1024]{2,1,0:T(8,128)(2,1)}, u32[]{:S(2)}, u32[]{:S(2)}) async-start(bf16[32,32,1024]{2,1,0:T(8,128)(2,1)} %bitcast.48), calls=%async_computation.2 | async-start | bytes 4194304 | tf_op jit(solution)/shard_map/all_to_all | solution.py:12
  108.6 2.4 fusion.22
  110.9 22.4 %all-gather.2.cloned.1.call-done = bf16[32,56,1024]{2,1,0:T(8,128)(2,1)} async-done(((bf16[2,56,1024]{2,1,0:T(8,128)(2,1)}), bf16[32,56,1024]{2,1,0:T(8,128)(2,1)}) %all-gather.2.cloned.1.call-update) | async-done | bytes 3670032 | tf_op jit(solution)/shard_map/all_gather | solution.py:53
  133.3 1.5 slice.32
  134.9 5.1 %fusion.53 = f32[1024,768]{1,0:T(8,128)} fusion(bf16[1024,1024]{1,0:T(8,128)(2,1)} %bitcast.4, bf16[1024,768]{1,0:T(8,128)(2,1)S(1)} %bitcast.52), kind=kOutput, calls=%fused_computation.84 | convolution fusion | flops 1610612736 | bytes 6815744 | tf_op jit(solution)/shard_map/dot_general | solution.py:91
  139.9 6.0 %fusion.12 = bf16[768,1024]{1,0:T(8,128)(2,1)} fusion(bf16[1024,1024]{1,0:T(8,128)(2,1)} %bitcast.18, f32[1024]{0:T(1024)S(1)} %fusion.22, f32[1024,768]{1,0:T(8,128)} %fusion.53), kind=kOutput, calls=%fused_computation.16 | convolution fusion | flops 1621622784 | bytes 6819840 | tf_op jit(solution)/shard_map/dot_general | solution.py:97
  147.4 5.4 %convolution_convert_fusion.2 = bf16[1024,1024]{1,0:T(8,128)(2,1)} fusion(bf16[768,1024]{1,0:T(8,128)(2,1)S(1)} %bitcast.50, f32[1024,768]{1,0:T(8,128)} %fusion.53), kind=kOutput, calls=%fused_computation.15 | convolution fusion | flops 1618739200 | bytes 6815744 | tf_op jit(solution)/shard_map/dot_general | solution.py:103
  152.7 16.4 %all-to-all-start.1 = ((bf16[32,32,1024]{2,1,0:T(8,128)(2,1)}), bf16[32,32,1024]{2,1,0:T(8,128)(2,1)}, u32[]{:S(2)}, u32[]{:S(2)}) async-start(bf16[32,32,1024]{2,1,0:T(8,128)(2,1)} %bitcast.51), calls=%async_computation.1 | async-start | bytes 4194304 | tf_op jit(solution)/shard_map/all_to_all | solution.py:12
  169.5 27.6 %all-to-all-done.1 = bf16[32,32,1024]{2,1,0:T(8,128)(2,1)} async-done(((bf16[32,32,1024]{2,1,0:T(8,128)(2,1)}), bf16[32,32,1024]{2,1,0:T(8,128)(2,1)}, u32[]{:S(2)}, u32[]{:S(2)}) %all-to-all-start.1) | async-done | bytes 2097184 | tf_op jit(solution)/shard_map/all_to_all | solution.py:12
  197.1 2.9 %convolution_bitcast_fusion = f32[128,1024]{1,0:T(8,128)} fusion(bf16[32,32,1024]{2,1,0:T(8,128)(2,1)} %all-to-all-done.1, f32[32,128]{1,0:T(8,128)S(1)} %fusion.26, s32[32,128]{1,0:T(8,128)S(1)} %fusion.27), kind=kOutput, calls=%fused_computation.18 | convolution fusion | flops 269484032 | bytes 2654208 | tf_op jit(solution)/shard_map/dot_general | solution.py:112
  200.0 14.3 %reduce-scatter.2.cloned.1.call-done = bf16[48,1024]{1,0:T(8,128)(2,1)} async-done(((bf16[768,1024]{1,0:T(8,128)(2,1)}), bf16[48,1024]{1,0:T(8,128)(2,1)}) %reduce-scatter.2.cloned.1.call-update) | async-done | bytes 98320 | tf_op jit(solution)/shard_map/reduce_scatter | solution.py:100
  215.1 20.4 %collective-permute-start.2 = (bf16[24,1024]{1,0:T(8,128)(2,1)S(1)}, bf16[24,1024]{1,0:T(8,128)(2,1)S(1)}, u32[]{:S(2)}, u32[]{:S(2)}) collective-permute-start(bf16[24,1024]{1,0:T(8,128)(2,1)S(1)} %get-tuple-element.8), channel_id=1, source_target_pairs={{0,16},{1,48},{2,80},{3,112},{4,144},{5,176},{6,208},{7,240},{8,27... | collective-permute-start | bytes 147464 | tf_op jit(solution)/shard_map/ppermute | solution.py:27
  235.5 6.1 %collective-permute-start.3 = (bf16[24,1024]{1,0:T(8,128)(2,1)S(1)}, bf16[24,1024]{1,0:T(8,128)(2,1)S(1)}, u32[]{:S(2)}, u32[]{:S(2)}) collective-permute-start(bf16[24,1024]{1,0:T(8,128)(2,1)S(1)} %get-tuple-element.9), channel_id=1, source_target_pairs={{0,0},{1,32},{2,64},{3,96},{4,128},{5,160},{6,192},{7,224},{8,256}... | collective-permute-start | bytes 147464 | tf_op jit(solution)/shard_map/ppermute | solution.py:27
  241.6 2.9 %fusion.17 = bf16[128,1024]{1,0:T(8,128)(2,1)} fusion(f32[128,1024]{1,0:T(8,128)S(1)} %get-tuple-element.11, f32[128,1024]{1,0:T(8,128)} %convolution_bitcast_fusion, bf16[32,32,1024]{2,1,0:T(8,128)(2,1)} %all-to-all-done.1, f32[32,128]{1,0:T(8,128)S(1)} %fusion.26, s32[32,128]{1,0:T(8,128)S(1)} %fusion.27), kind=kOutput, calls=%fused_computation.22 | convolution fusion | flops 269484032 | bytes 3440640 | tf_op jit(solution)/shard_map/dot_general | solution.py:110
  244.5 8.1 %collective-permute-done.3 = bf16[24,1024]{1,0:T(8,128)(2,1)S(1)} collective-permute-done((bf16[24,1024]{1,0:T(8,128)(2,1)S(1)}, bf16[24,1024]{1,0:T(8,128)(2,1)S(1)}, u32[]{:S(2)}, u32[]{:S(2)}) %collective-permute-start.3) | collective-permute-done | bytes 49184 | tf_op jit(solution)/shard_map/ppermute | solution.py:27
  (44 shorter events, 9.0 us)
Async XLA Ops:
  7.2 44.3 %copy-start = (bf16[1408,1024]{1,0:T(8,128)(2,1)S(1)}, bf16[1408,1024]{1,0:T(8,128)(2,1)}, u32[]{:S(2)}) copy-start(bf16[1408,1024]{1,0:T(8,128)(2,1)} %param.16) | copy-start | bytes 8650756
  7.2 42.7 %copy-start.1 = (bf16[128,1408]{1,0:T(8,128)(2,1)S(1)}, bf16[128,1408]{1,0:T(8,128)(2,1)}, u32[]{:S(2)}) copy-start(bf16[128,1408]{1,0:T(8,128)(2,1)} %param.12) | copy-start | bytes 1081348
  7.2 42.9 %copy-start.7 = (s32[128]{0:T(128)S(1)}, s32[128]{0:T(128)}, u32[]{:S(2)}) copy-start(s32[128]{0:T(128)} %param.13) | copy-start | bytes 1540
  7.2 126.1 %all-gather.2.cloned.1.call-start = ((), (), s32[]{:S(2)}) async-start(), calls=%async_computation.4 | async-start | bytes 3899392 | tf_op jit(solution)/shard_map/all_gather | solution.py:53
  8.4 27.7 %collective-permute-start = (bf16[56,1024]{1,0:T(8,128)(2,1)S(1)}, bf16[56,1024]{1,0:T(8,128)(2,1)S(1)}, u32[]{:S(2)}, u32[]{:S(2)}) collective-permute-start(bf16[56,1024]{1,0:T(8,128)(2,1)S(1)} %get-tuple-element.4), channel_id=1, source_target_pairs={{0,16},{1,48},{2,80},{3,112},{4,144},{5,176},{6,208},{7,240},{8,27... | collective-permute-start | bytes 344072 | tf_op jit(solution)/shard_map/ppermute | solution.py:27
  23.9 22.9 %collective-permute-start.1 = (bf16[56,1024]{1,0:T(8,128)(2,1)S(1)}, bf16[56,1024]{1,0:T(8,128)(2,1)S(1)}, u32[]{:S(2)}, u32[]{:S(2)}) collective-permute-start(bf16[56,1024]{1,0:T(8,128)(2,1)S(1)} %get-tuple-element.5), channel_id=1, source_target_pairs={{0,0},{1,32},{2,64},{3,96},{4,128},{5,160},{6,192},{7,224},{8,256}... | collective-permute-start | bytes 344072 | tf_op jit(solution)/shard_map/ppermute | solution.py:27
  49.8 3.4 %copy-start.3 = (f32[1024]{0:T(1024)S(1)}, f32[1024]{0:T(1024)}, u32[]{:S(2)}) copy-start(f32[1024]{0:T(1024)} %param.18) | copy-start | bytes 12292
  53.2 2.1 copy-start.5
  55.3 46.1 %all-to-all-start = ((bf16[32,32,1024]{2,1,0:T(8,128)(2,1)}), bf16[32,32,1024]{2,1,0:T(8,128)(2,1)}, u32[]{:S(2)}, u32[]{:S(2)}) async-start(bf16[32,32,1024]{2,1,0:T(8,128)(2,1)} %bitcast.49), calls=%async_computation | async-start | bytes 4194304 | tf_op jit(solution)/shard_map/all_to_all | solution.py:12
  76.7 31.9 %copy-start.2 = (bf16[1024,32]{0,1:T(8,128)(2,1)S(1)}, bf16[1024,32]{0,1:T(8,128)(2,1)}, u32[]{:S(2)}) copy-start(bf16[1024,32]{0,1:T(8,128)(2,1)} %param.19) | copy-start | bytes 196612
  101.4 38.5 %all-to-all-start.2 = ((bf16[32,32,1024]{2,1,0:T(8,128)(2,1)}), bf16[32,32,1024]{2,1,0:T(8,128)(2,1)}, u32[]{:S(2)}, u32[]{:S(2)}) async-start(bf16[32,32,1024]{2,1,0:T(8,128)(2,1)} %bitcast.48), calls=%async_computation.2 | async-start | bytes 4194304 | tf_op jit(solution)/shard_map/all_to_all | solution.py:12
  108.5 105.8 %reduce-scatter.2.cloned.1.call-start = ((), (), s32[]{:S(2)}) async-start(), calls=%async_computation.5 | async-start | bytes 1671168 | tf_op jit(solution)/shard_map/reduce_scatter | solution.py:100
  146.0 1.4 slice-start
  152.7 16.4 %copy-start.4 = (f32[1024]{0:T(1024)S(1)}, f32[1024]{0:T(1024)}, u32[]{:S(2)}) copy-start(f32[1024]{0:T(1024)} %param.18) | copy-start | bytes 12292
  152.7 16.4 %copy-start.6 = (f32[128]{0:T(128)S(1)}, f32[128]{0:T(128)}, u32[]{:S(2)}) copy-start(f32[128]{0:T(128)} %copy-done.5) | copy-start | bytes 1540
  152.7 44.3 %all-to-all-start.1 = ((bf16[32,32,1024]{2,1,0:T(8,128)(2,1)}), bf16[32,32,1024]{2,1,0:T(8,128)(2,1)}, u32[]{:S(2)}, u32[]{:S(2)}) async-start(bf16[32,32,1024]{2,1,0:T(8,128)(2,1)} %bitcast.51), calls=%async_computation.1 | async-start | bytes 4194304 | tf_op jit(solution)/shard_map/all_to_all | solution.py:12
  215.1 29.4 %collective-permute-start.2 = (bf16[24,1024]{1,0:T(8,128)(2,1)S(1)}, bf16[24,1024]{1,0:T(8,128)(2,1)S(1)}, u32[]{:S(2)}, u32[]{:S(2)}) collective-permute-start(bf16[24,1024]{1,0:T(8,128)(2,1)S(1)} %get-tuple-element.8), channel_id=1, source_target_pairs={{0,16},{1,48},{2,80},{3,112},{4,144},{5,176},{6,208},{7,240},{8,27... | collective-permute-start | bytes 147464 | tf_op jit(solution)/shard_map/ppermute | solution.py:27
  235.5 17.1 %collective-permute-start.3 = (bf16[24,1024]{1,0:T(8,128)(2,1)S(1)}, bf16[24,1024]{1,0:T(8,128)(2,1)S(1)}, u32[]{:S(2)}, u32[]{:S(2)}) collective-permute-start(bf16[24,1024]{1,0:T(8,128)(2,1)S(1)} %get-tuple-element.9), channel_id=1, source_target_pairs={{0,0},{1,32},{2,64},{3,96},{4,128},{5,160},{6,192},{7,224},{8,256}... | collective-permute-start | bytes 147464 | tf_op jit(solution)/shard_map/ppermute | solution.py:27
Sparse Core Ops, SparseCore 0:
  47.7 85.6 all-gather.1
  146.1 68.1 reduce-scatter.1

commit v2 on v1

v2 whole, which is shorter than its diff:
```python
import jax
import jax.numpy as jnp
from jax import lax
from jax.experimental import pallas as pl
from jax.experimental.pallas import tpu as pltpu
from jax.sharding import PartitionSpec as P

EXPERTS = 32
TOPK = 6
CAP = 32
PLANES = 16
CHIPS = 16
UP_ROWS = 32
PACK_ROWS = 48
STRIDE = 3
AXES = ("dp", "expert")


def home(plane, k):
    return plane ^ (10 * k)


def moves(flip, back):
    perm = []
    for chip in range(CHIPS):
        for core in range(2):
            for z in range(PLANES):
                k = core ^ flip
                here = (2 * chip + core) * PLANES + z
                there = (2 * home(z, k) + k) * PLANES + (chip + STRIDE * z) % PLANES
                perm.append((there, here) if back else (here, there))
    return perm


def swap(pair, odd, back):
    same, other = jnp.where(odd, pair[1], pair[0]), jnp.where(odd, pair[0], pair[1])
    return (
        lax.ppermute(same, AXES, moves(0, back)),
        lax.ppermute(other, AXES, moves(1, back)),
    )


def exchange(rows):
    return lax.all_to_all(rows, "dp", split_axis=0, concat_axis=0, tiled=True)


def hidden_kernel(info, w_ref, x_ref, cot_ref, router_ref, hid_ref, grad_ref, up_ref, gated_ref):
    first, odd, expert = info[0], info[1], info[2]
    f32, bf16 = jnp.float32, jnp.bfloat16
    cols = up_ref.shape[1]
    for block in range(2 * CHIPS):
        at = lax.rem(first + block // 2, PLANES)
        slot = (odd + block) & 1
        up_ref[block * UP_ROWS : (block + 1) * UP_ROWS, :] = w_ref[at, slot, :UP_ROWS, :cols]
    rows = x_ref.shape[0]
    step = 256
    for start in range(0, rows, step):
        part = pl.ds(start, step)
        x = x_ref[part, :]
        pre = jnp.dot(x, up_ref[...], preferred_element_type=f32)
        hid_ref[part, :] = jax.nn.gelu(pre, approximate=True).astype(bf16)
        gates = jax.nn.sigmoid(jnp.dot(x, router_ref[...], preferred_element_type=f32))
        mine = lax.broadcasted_iota(jnp.int32, gates.shape, 1) == expert
        gate = jnp.sum(jnp.where(mine, gates, 0.0), axis=1, keepdims=True)
        gated_ref[part, :] = (gate * cot_ref[part, :].astype(f32)).astype(bf16)
    group = grad_ref.shape[1]
    half = PLANES // 2
    for j in range(2):
        grad = lax.dot_general(
            hid_ref[:, j * half * group : (j + 1) * half * group],
            gated_ref[...],
            (((0,), (0,)), ((), ())),
            preferred_element_type=f32,
        ).astype(bf16)
        for i in range(half):
            at = lax.rem(first + j * half + i, PLANES)
            grad_ref[at] = grad[i * group : (i + 1) * group, :]


def out_kernel(info, w_ref, hid_ref, out_ref, wide_ref, down_ref):
    first, odd = info[0], info[1]
    cols = hid_ref.shape[1]
    width = out_ref.shape[1]
    spare = width - cols
    full = PACK_ROWS - UP_ROWS
    tail = UP_ROWS * spare // width
    for block in range(2 * CHIPS):
        at = lax.rem(first + block // 2, PLANES)
        slot = (odd + block) & 1
        base = block * (full + tail)
        wide_ref[base : base + full, :] = w_ref[at, slot, UP_ROWS:PACK_ROWS, :].astype(jnp.float32)
        rest = w_ref[at, slot, :UP_ROWS, cols:].astype(jnp.float32)
        for q in range(UP_ROWS // tail):
            wide_ref[base + full : base + full + tail, q * spare : (q + 1) * spare] = rest[
                q * tail : (q + 1) * tail, :
            ]
    down_ref[...] = wide_ref[...].astype(jnp.bfloat16)
    rows = hid_ref.shape[0]
    step = 256
    for start in range(0, rows, step):
        part = pl.ds(start, step)
        out_ref[part, :] = jnp.dot(
            hid_ref[part, :], down_ref[...], preferred_element_type=jnp.float32
        ).astype(jnp.bfloat16)


def per_device(
    enc_out,
    actions,
    enc_gain,
    enc_bias,
    embed_w,
    action_table,
    pred_gain,
    router_w,
    up_w,
    down_w,
    cotangent,
    routes,
):
    bf16, f32 = jnp.bfloat16, jnp.float32
    tokens, width = cotangent.shape
    up_cols = up_w.shape[2]
    hid_rows = down_w.shape[1]
    device = lax.axis_index("dp")
    chip, core = device // 2, device % 2
    odd = core == 1
    plane = jnp.where(odd, chip ^ 10, chip)
    info = jnp.stack([STRIDE * plane % PLANES, core, 2 * plane + core]).astype(jnp.int32)

    spare = width - up_cols
    full = PACK_ROWS - UP_ROWS
    rest = down_w[:, full:, :].reshape(2, hid_rows - full, width // spare, spare)
    rest = rest.transpose(0, 2, 1, 3).reshape(2, UP_ROWS, spare)
    packed = jnp.concatenate(
        [jnp.concatenate([up_w, rest], axis=2), down_w[:, :full, :]], axis=1
    )
    weights = lax.all_gather(
        jnp.stack(swap(packed, odd, False)), "expert", axis=0, tiled=True
    ).reshape(PLANES, 2, PACK_ROWS, width)

    names = [2 * home(d // 2, d % 2) + d % 2 for d in range(EXPERTS)]
    experts = jnp.array(names, dtype=jnp.int32)
    hits = jnp.sum((routes.T[:, None, :] == experts[None, :, None]).astype(f32), axis=0)
    order = jnp.arange(tokens, dtype=jnp.int32)
    earlier = (order[:, None] < order[None, :]).astype(bf16)
    rank = jnp.dot(hits.astype(bf16), earlier, preferred_element_type=f32)
    place = jnp.where(hits > 0.0, rank.astype(jnp.int32), -1)
    slots = jnp.arange(CAP, dtype=jnp.int32)
    pick = (place[:, None, :] == slots[None, :, None]).reshape(EXPERTS * CAP, tokens)
    pick = pick.astype(bf16)

    got_cot = exchange(jnp.dot(pick, cotangent, preferred_element_type=f32).astype(bf16))

    encoded = enc_out.astype(f32)
    center = encoded - jnp.mean(encoded, axis=-1, keepdims=True)
    spread = jnp.mean(center * center, axis=-1, keepdims=True)
    normed = (center * lax.rsqrt(spread + 1e-06) * enc_gain + enc_bias).astype(bf16)
    onehot = (
        actions[:, None] == jnp.arange(action_table.shape[0], dtype=jnp.int32)[None, :]
    ).astype(bf16)
    residual = jnp.dot(normed, embed_w, preferred_element_type=f32) + jnp.dot(
        onehot, action_table, preferred_element_type=f32
    )
    scaled = (
        residual
        * lax.rsqrt(jnp.mean(residual * residual, axis=-1, keepdims=True) + 1e-06)
        * pred_gain
    ).astype(bf16)
    got_tok = exchange(jnp.dot(pick, scaled, preferred_element_type=f32).astype(bf16))

    slots_all = EXPERTS * CAP
    smem = pl.BlockSpec(memory_space=pltpu.SMEM)
    vmem = pl.BlockSpec(memory_space=pltpu.VMEM)
    group = 2 * hid_rows
    hidden, grad = pl.pallas_call(
        hidden_kernel,
        out_shape=(
            jax.ShapeDtypeStruct((slots_all, up_cols), bf16),
            jax.ShapeDtypeStruct((PLANES, group, width), bf16),
        ),
        in_specs=[smem, vmem, vmem, vmem, vmem],
        out_specs=(vmem, vmem),
        scratch_shapes=[
            pltpu.VMEM((width, up_cols), bf16),
            pltpu.VMEM((slots_all, width), bf16),
        ],
        cost_estimate=pl.CostEstimate(
            flops=4 * slots_all * width * up_cols,
            bytes_accessed=11 << 20,
            transcendentals=slots_all * up_cols,
        ),
    )(info, weights, got_tok, got_cot, router_w)
    summed = lax.psum_scatter(grad, "expert", scatter_dimension=0, tiled=True)
    same, other = swap(summed.reshape(2, hid_rows, width), odd, True)
    grad_down = jnp.stack([jnp.where(odd, other, same), jnp.where(odd, same, other)])

    expert_out = pl.pallas_call(
        out_kernel,
        out_shape=jax.ShapeDtypeStruct((slots_all, width), bf16),
        in_specs=[smem, vmem, vmem],
        out_specs=vmem,
        scratch_shapes=[
            pltpu.VMEM((up_cols, width), f32),
            pltpu.VMEM((up_cols, width), bf16),
        ],
        cost_estimate=pl.CostEstimate(
            flops=2 * slots_all * width * up_cols,
            bytes_accessed=7 << 20,
            transcendentals=0,
        ),
    )(info, weights, hidden)
    returned = exchange(expert_out)
    logits = lax.dot_general(
        router_w, scaled, (((0,), (1,)), ((), ())), preferred_element_type=f32
    )
    gates = jnp.stack([logits[name] for name in names])
    gates = jax.nn.sigmoid(gates)
    weight = pick.reshape(EXPERTS, CAP, tokens).astype(f32) * gates[:, None, :]
    weight = weight.reshape(slots_all, tokens)
    coarse = weight.astype(bf16)
    fine = (weight - coarse.astype(f32)).astype(bf16)
    dims = (((0,), (0,)), ((), ()))
    combined = lax.dot_general(
        coarse, returned, dims, preferred_element_type=f32
    ) + lax.dot_general(fine, returned, dims, preferred_element_type=f32)
    predicted = (residual + combined).astype(bf16)
    return (predicted, grad_down)


def solution(mesh):
    placed = (
        P(("dp", "expert"), None),
        P(("dp", "expert")),
        P(),
        P(),
        P(),
        P(),
        P(),
        P(),
        P("expert", "dp", None),
        P("expert", "dp", None),
        P(("dp", "expert"), None),
        P(("dp", "expert"), None),
    )
    return jax.shard_map(
        per_device,
        mesh=mesh,
        in_specs=placed,
        out_specs=(P(("dp", "expert"), None), P("expert", "dp", None)),
        check_vma=False,
    )
```

time: 261 us -> 230 us (0.88)
  the two profiles are of different devices: /device:TPU:81 before, /device:TPU:69 now
where the time goes in v2:
time: 230 us; the launch traced here: 229 us
  waiting for transfers between devices  110 us (48%)
  starting transfers between devices  67.4 us (29%)
  between operations  14.3 us (6%)
  Pallas kernels  14.2 us (6%)
  matrix products  14.1 us (6%)
  other arithmetic  5.17 us (2%)
  local copies, waits for them, and re-layouts  4.17 us (2%)
    all_to_all x3, waiting for transfers between devices, exchange(): return lax.all_to_all(rows, 'dp', split_axis=0, concat_axis=0, tiled=True)  73 us
    ppermute x2, starting transfers between devices, swap(): lax.ppermute(other, AXES, moves(1, back))  33.7 us
    all_to_all x3, starting transfers between devices, exchange(): return lax.all_to_all(rows, 'dp', split_axis=0, concat_axis=0, tiled=True)  24.6 us
    ppermute x2, waiting for transfers between devices, swap(): lax.ppermute(same, AXES, moves(0, back))  17.6 us
    reduce_scatter x1, waiting for transfers between devices, per_device(): summed = lax.psum_scatter(grad, 'expert', scatter_dimension=0, tiled=True)  17 us
    ppermute x2, starting transfers between devices, swap(): lax.ppermute(same, AXES, moves(0, back))  9.07 us
    pallas_call x1, Pallas kernels, per_device(): pl.pallas_call(hidden_kernel, out_shape=(jax.ShapeDtypeStruct((slots_all,...  8.67 us
    pallas_call x1, Pallas kernels, per_device(): pl.pallas_call(out_kernel, out_shape=jax.ShapeDtypeStruct((slots_all, wid...  5.53 us
  transfers between devices with their start and end apart: 9, of which 7 were waited for; matrix products, arithmetic and copies ran while one was open for 8% of the time, Pallas kernels for 2%

profile of v2, /device:TPU:69, one launch (start us, length us, event | category | flops | bytes accessed | tf_op | source)
XLA Modules:
  0.0 229.3 jit_solution(12493754302947558727)
XLA Ops:
  7.3 1.0 slice.153
  9.0 0.9 pad_maximum_fusion
  10.0 13.3 %collective-permute-start.1 = (bf16[48,1024]{1,0:T(8,128)(2,1)S(1)}, bf16[48,1024]{1,0:T(8,128)(2,1)S(1)}, u32[]{:S(2)}, u32[]{:S(2)}) collective-permute-start(bf16[48,1024]{1,0:T(8,128)(2,1)S(1)} %get-tuple-element.7), channel_id=1, source_target_pairs={{0,336},{1,371},{2,278},{3,313},{4,476},{5,511},{6,402},{7,437},{8... | collective-permute-start | bytes 294920 | tf_op jit(solution)/shard_map/ppermute | solution.py:39
  23.3 3.9 %collective-permute-start = (bf16[48,1024]{1,0:T(8,128)(2,1)S(1)}, bf16[48,1024]{1,0:T(8,128)(2,1)S(1)}, u32[]{:S(2)}, u32[]{:S(2)}) collective-permute-start(bf16[48,1024]{1,0:T(8,128)(2,1)S(1)} %get-tuple-element.6), channel_id=1, source_target_pairs={{0,0},{1,35},{2,70},{3,105},{4,140},{5,175},{6,194},{7,229},{8,264... | collective-permute-start | bytes 294920 | tf_op jit(solution)/shard_map/ppermute | solution.py:38
  28.0 2.4 %collective-permute-done.1 = bf16[48,1024]{1,0:T(8,128)(2,1)S(1)} collective-permute-done((bf16[48,1024]{1,0:T(8,128)(2,1)S(1)}, bf16[48,1024]{1,0:T(8,128)(2,1)S(1)}, u32[]{:S(2)}, u32[]{:S(2)}) %collective-permute-start.1) | collective-permute-done | bytes 98336 | tf_op jit(solution)/shard_map/ppermute | solution.py:39
  30.3 8.5 %collective-permute-done = bf16[48,1024]{1,0:T(8,128)(2,1)S(1)} collective-permute-done((bf16[48,1024]{1,0:T(8,128)(2,1)S(1)}, bf16[48,1024]{1,0:T(8,128)(2,1)S(1)}, u32[]{:S(2)}, u32[]{:S(2)}) %collective-permute-start) | collective-permute-done | bytes 98336 | tf_op jit(solution)/shard_map/ppermute | solution.py:38
  40.4 1.3 fusion.22
  41.7 1.4 multiply_reduce_fusion
  43.2 2.1 convolution_convert_fusion.1
  45.4 7.6 %all-to-all-start = ((bf16[32,32,1024]{2,1,0:T(8,128)(2,1)}), bf16[32,32,1024]{2,1,0:T(8,128)(2,1)}, u32[]{:S(2)}, u32[]{:S(2)}) async-start(bf16[32,32,1024]{2,1,0:T(8,128)(2,1)} %bitcast.53), calls=%async_computation | async-start | bytes 4194304 | tf_op jit(solution)/shard_map/all_to_all | solution.py:44
  53.0 3.0 %convolution_convert_fusion = bf16[1024,1024]{1,0:T(8,128)(2,1)} fusion(pred[1024,128]{1,0:T(32,128)(4,1)S(1)} %bitcast_compare_fusion, bf16[128,1024]{1,0:T(8,128)(2,1)} %param.23), kind=kOutput, calls=%fused_computation | convolution fusion | flops 269484032 | bytes 2490368 | tf_op jit(solution)/shard_map/dot_general | solution.py:153
  56.0 23.4 %all-to-all-done = bf16[32,32,1024]{2,1,0:T(8,128)(2,1)} async-done(((bf16[32,32,1024]{2,1,0:T(8,128)(2,1)}), bf16[32,32,1024]{2,1,0:T(8,128)(2,1)}, u32[]{:S(2)}, u32[]{:S(2)}) %all-to-all-start) | async-done | bytes 2097184 | tf_op jit(solution)/shard_map/all_to_all | solution.py:44
  79.4 8.4 %all-to-all-start.1 = ((bf16[32,32,1024]{2,1,0:T(8,128)(2,1)}), bf16[32,32,1024]{2,1,0:T(8,128)(2,1)}, u32[]{:S(2)}, u32[]{:S(2)}) async-start(bf16[32,32,1024]{2,1,0:T(8,128)(2,1)} %bitcast.52), calls=%async_computation.1 | async-start | bytes 4194304 | tf_op jit(solution)/shard_map/all_to_all | solution.py:44
  89.4 24.9 %all-to-all-done.1 = bf16[32,32,1024]{2,1,0:T(8,128)(2,1)} async-done(((bf16[32,32,1024]{2,1,0:T(8,128)(2,1)}), bf16[32,32,1024]{2,1,0:T(8,128)(2,1)}, u32[]{:S(2)}, u32[]{:S(2)}) %all-to-all-start.1) | async-done | bytes 2097184 | tf_op jit(solution)/shard_map/all_to_all | solution.py:44
  114.3 8.7 %shard_map.140 = (bf16[1024,768]{1,0:T(8,128)(2,1)}, bf16[16,48,1024]{2,1,0:T(8,128)(2,1)}) custom-call(s32[3]{0:T(128)} %pad_add_fusion.info, bf16[16,2,48,1024]{3,2,1,0:T(8,128)(2,1)} %bitcast.54, bf16[1024,1024]{1,0:T(8,128)(2,1)} %bitcast.15.x_ref, bf16[1024,1024]{1,0:T(8,128)(2,1)} %bitcast.17.cot_ref, bf16[1024,32]{1,0:T(8,128)(2,1)} %copy.17.router_ref), custom_call_target="tpu_custom_call" | custom-call | flops 3221225472 | bytes 11534336 | tf_op jit(solution)/shard_map/pallas_call | solution.py:176
  123.0 5.5 %shard_map.141 = bf16[1024,1024]{1,0:T(8,128)(2,1)} custom-call(s32[3]{0:T(128)} %pad_add_fusion.info, bf16[16,2,48,1024]{3,2,1,0:T(8,128)(2,1)} %bitcast.55, bf16[1024,768]{1,0:T(8,128)(2,1)} %get-tuple-element.4.hid_ref), custom_call_target="tpu_custom_call" | custom-call | flops 1610612736 | bytes 7340032 | tf_op jit(solution)/shard_map/pallas_call | solution.py:198
  128.6 8.5 %all-to-all-start.2 = ((bf16[32,32,1024]{2,1,0:T(8,128)(2,1)}), bf16[32,32,1024]{2,1,0:T(8,128)(2,1)}, u32[]{:S(2)}, u32[]{:S(2)}) async-start(bf16[32,32,1024]{2,1,0:T(8,128)(2,1)} %bitcast.51), calls=%async_computation.2 | async-start | bytes 4194304 | tf_op jit(solution)/shard_map/all_to_all | solution.py:44
  138.8 24.8 %all-to-all-done.2 = bf16[32,32,1024]{2,1,0:T(8,128)(2,1)} async-done(((bf16[32,32,1024]{2,1,0:T(8,128)(2,1)}), bf16[32,32,1024]{2,1,0:T(8,128)(2,1)}, u32[]{:S(2)}, u32[]{:S(2)}) %all-to-all-start.2) | async-done | bytes 2097184 | tf_op jit(solution)/shard_map/all_to_all | solution.py:44
  163.5 2.9 %convolution_bitcast_fusion = f32[128,1024]{1,0:T(8,128)} fusion(bf16[32,32,1024]{2,1,0:T(8,128)(2,1)} %all-to-all-done.2, f32[32,128]{1,0:T(8,128)S(1)} %add_divide_fusion, s32[32,128]{1,0:T(8,128)S(1)} %fusion.3), kind=kOutput, calls=%fused_computation.3 | convolution fusion | flops 269484032 | bytes 2654208 | tf_op jit(solution)/shard_map/dot_general | solution.py:226
  166.5 17.0 %reduce-scatter.2.cloned.1.call-done = bf16[1,48,1024]{2,1,0:T(8,128)(2,1)} async-done(((bf16[16,48,1024]{2,1,0:T(8,128)(2,1)}), bf16[1,48,1024]{2,1,0:T(8,128)(2,1)}) %reduce-scatter.2.cloned.1.call-update) | async-done | bytes 98320 | tf_op jit(solution)/shard_map/reduce_scatter | solution.py:194
  184.3 20.4 %collective-permute-start.2 = (bf16[24,1024]{1,0:T(8,128)(2,1)S(1)}, bf16[24,1024]{1,0:T(8,128)(2,1)S(1)}, u32[]{:S(2)}, u32[]{:S(2)}) collective-permute-start(bf16[24,1024]{1,0:T(8,128)(2,1)S(1)} %get-tuple-element.10), channel_id=1, source_target_pairs={{336,0},{371,1},{278,2},{313,3},{476,4},{511,5},{402,6},{437,7},{8... | collective-permute-start | bytes 147464 | tf_op jit(solution)/shard_map/ppermute | solution.py:39
  204.7 5.1 %collective-permute-start.3 = (bf16[24,1024]{1,0:T(8,128)(2,1)S(1)}, bf16[24,1024]{1,0:T(8,128)(2,1)S(1)}, u32[]{:S(2)}, u32[]{:S(2)}) collective-permute-start(bf16[24,1024]{1,0:T(8,128)(2,1)S(1)} %get-tuple-element.11), channel_id=1, source_target_pairs={{0,0},{35,1},{70,2},{105,3},{140,4},{175,5},{194,6},{229,7},{264,8... | collective-permute-start | bytes 147464 | tf_op jit(solution)/shard_map/ppermute | solution.py:38
  209.9 2.9 %fusion.2 = bf16[128,1024]{1,0:T(8,128)(2,1)} fusion(f32[128,1024]{1,0:T(8,128)S(1)} %get-tuple-element.45, f32[128,1024]{1,0:T(8,128)} %convolution_bitcast_fusion, bf16[32,32,1024]{2,1,0:T(8,128)(2,1)} %all-to-all-done.2, f32[32,128]{1,0:T(8,128)S(1)} %add_divide_fusion, s32[32,128]{1,0:T(8,128)S(1)} %fusion.3), kind=kOutput, calls=%fused_computation.7 | convolution fusion | flops 269484032 | bytes 3440640 | tf_op jit(solution)/shard_map/dot_general | solution.py:224
  212.7 9.1 %collective-permute-done.3 = bf16[24,1024]{1,0:T(8,128)(2,1)S(1)} collective-permute-done((bf16[24,1024]{1,0:T(8,128)(2,1)S(1)}, bf16[24,1024]{1,0:T(8,128)(2,1)S(1)}, u32[]{:S(2)}, u32[]{:S(2)}) %collective-permute-start.3) | collective-permute-done | bytes 49184 | tf_op jit(solution)/shard_map/ppermute | solution.py:38
  (47 shorter events, 7.9 us)
Async XLA Ops:
  7.2 34.5 %copy-start = (bf16[1408,1024]{1,0:T(8,128)(2,1)S(1)}, bf16[1408,1024]{1,0:T(8,128)(2,1)}, u32[]{:S(2)}) copy-start(bf16[1408,1024]{1,0:T(8,128)(2,1)} %param.17) | copy-start | bytes 8650756
  7.2 32.8 %copy-start.1 = (bf16[128,1408]{1,0:T(8,128)(2,1)S(1)}, bf16[128,1408]{1,0:T(8,128)(2,1)}, u32[]{:S(2)}) copy-start(bf16[128,1408]{1,0:T(8,128)(2,1)} %param.13) | copy-start | bytes 1081348
  7.2 33.2 %copy-start.8 = (s32[128]{0:T(128)S(1)}, s32[128]{0:T(128)}, u32[]{:S(2)}) copy-start(s32[128]{0:T(128)} %param.14) | copy-start | bytes 1540
  7.2 107.1 %all-gather.2.cloned.1.call-start = ((), (), s32[]{:S(2)}) async-start(), calls=%async_computation.4 | async-start | bytes 3342336 | tf_op jit(solution)/shard_map/all_gather | solution.py:138
  10.0 20.4 %collective-permute-start.1 = (bf16[48,1024]{1,0:T(8,128)(2,1)S(1)}, bf16[48,1024]{1,0:T(8,128)(2,1)S(1)}, u32[]{:S(2)}, u32[]{:S(2)}) collective-permute-start(bf16[48,1024]{1,0:T(8,128)(2,1)S(1)} %get-tuple-element.7), channel_id=1, source_target_pairs={{0,336},{1,371},{2,278},{3,313},{4,476},{5,511},{6,402},{7,437},{8... | collective-permute-start | bytes 294920 | tf_op jit(solution)/shard_map/ppermute | solution.py:39
  23.3 15.6 %collective-permute-start = (bf16[48,1024]{1,0:T(8,128)(2,1)S(1)}, bf16[48,1024]{1,0:T(8,128)(2,1)S(1)}, u32[]{:S(2)}, u32[]{:S(2)}) collective-permute-start(bf16[48,1024]{1,0:T(8,128)(2,1)S(1)} %get-tuple-element.6), channel_id=1, source_target_pairs={{0,0},{1,35},{2,70},{3,105},{4,140},{5,175},{6,194},{7,229},{8,264... | collective-permute-start | bytes 294920 | tf_op jit(solution)/shard_map/ppermute | solution.py:38
  39.8 2.0 copy-start.2
  41.7 1.5 copy-start.4
  43.2 2.2 copy-start.6
  45.4 34.0 %all-to-all-start = ((bf16[32,32,1024]{2,1,0:T(8,128)(2,1)}), bf16[32,32,1024]{2,1,0:T(8,128)(2,1)}, u32[]{:S(2)}, u32[]{:S(2)}) async-start(bf16[32,32,1024]{2,1,0:T(8,128)(2,1)} %bitcast.53), calls=%async_computation | async-start | bytes 4194304 | tf_op jit(solution)/shard_map/all_to_all | solution.py:44
  79.4 8.5 %copy-start.3 = (bf16[1024,32]{0,1:T(8,128)(2,1)S(1)}, bf16[1024,32]{0,1:T(8,128)(2,1)}, u32[]{:S(2)}) copy-start(bf16[1024,32]{0,1:T(8,128)(2,1)} %param.20) | copy-start | bytes 196612
  79.4 34.9 %all-to-all-start.1 = ((bf16[32,32,1024]{2,1,0:T(8,128)(2,1)}), bf16[32,32,1024]{2,1,0:T(8,128)(2,1)}, u32[]{:S(2)}, u32[]{:S(2)}) async-start(bf16[32,32,1024]{2,1,0:T(8,128)(2,1)} %bitcast.52), calls=%async_computation.1 | async-start | bytes 4194304 | tf_op jit(solution)/shard_map/all_to_all | solution.py:44
  87.9 95.6 %reduce-scatter.2.cloned.1.call-start = ((), (), s32[]{:S(2)}) async-start(), calls=%async_computation.5 | async-start | bytes 1671168 | tf_op jit(solution)/shard_map/reduce_scatter | solution.py:194
  128.6 8.5 %copy-start.5 = (f32[1024]{0:T(1024)S(1)}, f32[1024]{0:T(1024)}, u32[]{:S(2)}) copy-start(f32[1024]{0:T(1024)} %param.19) | copy-start | bytes 12292
  128.6 8.5 %copy-start.7 = (f32[128]{0:T(128)S(1)}, f32[128]{0:T(128)}, u32[]{:S(2)}) copy-start(f32[128]{0:T(128)} %copy-done.6) | copy-start | bytes 1540
  128.6 35.0 %all-to-all-start.2 = ((bf16[32,32,1024]{2,1,0:T(8,128)(2,1)}), bf16[32,32,1024]{2,1,0:T(8,128)(2,1)}, u32[]{:S(2)}, u32[]{:S(2)}) async-start(bf16[32,32,1024]{2,1,0:T(8,128)(2,1)} %bitcast.51), calls=%async_computation.2 | async-start | bytes 4194304 | tf_op jit(solution)/shard_map/all_to_all | solution.py:44
  184.3 28.4 %collective-permute-start.2 = (bf16[24,1024]{1,0:T(8,128)(2,1)S(1)}, bf16[24,1024]{1,0:T(8,128)(2,1)S(1)}, u32[]{:S(2)}, u32[]{:S(2)}) collective-permute-start(bf16[24,1024]{1,0:T(8,128)(2,1)S(1)} %get-tuple-element.10), channel_id=1, source_target_pairs={{336,0},{371,1},{278,2},{313,3},{476,4},{511,5},{402,6},{437,7},{8... | collective-permute-start | bytes 147464 | tf_op jit(solution)/shard_map/ppermute | solution.py:39
  204.7 17.1 %collective-permute-start.3 = (bf16[24,1024]{1,0:T(8,128)(2,1)S(1)}, bf16[24,1024]{1,0:T(8,128)(2,1)S(1)}, u32[]{:S(2)}, u32[]{:S(2)}) collective-permute-start(bf16[24,1024]{1,0:T(8,128)(2,1)S(1)} %get-tuple-element.11), channel_id=1, source_target_pairs={{0,0},{35,1},{70,2},{105,3},{140,4},{175,5},{194,6},{229,7},{264,8... | collective-permute-start | bytes 147464 | tf_op jit(solution)/shard_map/ppermute | solution.py:38
Sparse Core Ops, SparseCore 0:
  39.7 65.3 all-gather.1
  123.2 60.2 reduce-scatter.1
